TPU v7x, 32 devices: a whole 2x2x4 slice. The times are simulated.
32 devices in a mesh: tm: 16 (over z, y, x), tile: 2 (over core).
Axes of the slice: x: 2, y: 2, z: 4, core: 2. Of those that a mesh axis runs over, the one named last changes fastest.
Arguments:
- prior_space: float32 [1536, 1536], P('tile'), as said below
- node_gain: float32 [1536], replicated, may hold values from 0.4 to 1
- time_diag: float32 [32], P('tm'), may hold values from 0.6 to 1.5
- rho: float32 [32], P('tm'), may hold values from 0.2 to 0.95
- obs_values: float32 [2, 512, 16, 768], P('tile', 'tm'), may hold values from -1 to 1
- obs_weight: float32 [2, 512, 16], P('tile', 'tm'), may hold values from 0.25 to 4
- obs_step: int32 [2, 16, 32], P('tile', 'tm'), may hold values from 0 to 31, each once within a row
Outputs:
- separator_block: float32 [16, 1536, 1536], P('tm', 'tile')
- separator_coupling: float32 [16, 1536, 1536], P('tm', 'tile')
- interior_logdet: float32 [16], P('tm')
Inputs may be any that keep to these rules, and one draw needn't show every extreme that they name: prior_space is symmetric and each diagonal entry exceeds the sum of magnitudes of the other entries of its row. For each node block c and each index m of tm, obs_step[c, m] names every time step exactly once.
All inputs are finite; a program needn't handle non-finite values.
Results may differ from a plain program's by a relative error of at most 0.00013.
Values sent between devices are 32-bit elements; how exact they have to be, the bound alone decides.
A program may use at most 192 MiB of HBM per device.

v0:
```python
import jax
import jax.numpy as jnp
from jax import lax
from jax.sharding import PartitionSpec as P


def from_root(value, axis, source):
    kept = jnp.where(lax.axis_index(axis) == source, value, 0).astype(value.dtype)
    return lax.psum(kept, axis)


def from_behind(block, axis, distance):
    devices = range(lax.axis_size(axis))
    route = [(i - distance, i) for i in devices if i - distance in devices]
    return lax.ppermute(block, axis, route)


def gram_of(exchanged):
    tile_values, tile_weights = exchanged
    weighted = tile_values * tile_weights[..., None]
    return jnp.einsum("skrb,skrc->kbc", weighted, tile_values, precision=lax.Precision.HIGHEST)


def on_device(prior_space, node_gain, time_diag, rho, obs_values, obs_weight, obs_step):
    precise = lax.Precision.HIGHEST
    rows_of_block = prior_space.shape[0]
    node_count = prior_space.shape[1]
    count_of_tiles = lax.axis_size("tile")
    part_count = lax.axis_size("tm")
    index_of_tile = lax.axis_index("tile")
    row_start = index_of_tile * rows_of_block
    tile_values = obs_values[0]
    tile_weights = obs_weight[0]
    tile_steps = obs_step[0, 0]
    tile_total = tile_steps.shape[0]
    obs_rows = tile_values.shape[1]
    send_values = (
        jnp.zeros((tile_total, obs_rows, rows_of_block), jnp.float32)
        .at[tile_steps]
        .set(tile_values)
    )
    send_weights = jnp.zeros((tile_total, obs_rows), jnp.float32).at[tile_steps].set(tile_weights)
    send_values = send_values.reshape(part_count, 2, obs_rows, rows_of_block)
    send_weights = send_weights.reshape(part_count, 2, obs_rows)
    obs_grams = gram_of(
        (
            lax.all_to_all(send_values, "tm", split_axis=0, concat_axis=0, tiled=True),
            lax.all_to_all(send_weights, "tm", split_axis=0, concat_axis=0, tiled=True),
        )
    )

    def assemble(coef, gram_step):
        scaled_rows = coef * prior_space
        diag_part = lax.dynamic_slice_in_dim(scaled_rows, row_start, rows_of_block, 1) + gram_step
        return lax.dynamic_update_slice_in_dim(scaled_rows, diag_part, row_start, 1)

    interior = assemble(time_diag[0], obs_grams[0])
    separator = assemble(time_diag[1], obs_grams[1])
    own_gain = lax.dynamic_slice_in_dim(node_gain, row_start, rows_of_block)
    gain_tile = jnp.eye(rows_of_block, dtype=jnp.float32) * own_gain[None, :]
    trailing_matrix = interior
    schur_rows = jnp.zeros((rows_of_block, node_count), jnp.float32)
    log_total = jnp.zeros((), jnp.float32)
    for elimination_round in range(count_of_tiles):
        diag_tile = lax.dynamic_slice_in_dim(trailing_matrix, row_start, rows_of_block, 1)
        lower_factor = jnp.linalg.cholesky(diag_tile)
        seeded = lax.dynamic_update_slice_in_dim(trailing_matrix, gain_tile, row_start, 1)
        rows_solved = lax.linalg.triangular_solve(lower_factor, seeded, left_side=True, lower=True)
        log_total = log_total + jnp.where(
            index_of_tile == elimination_round,
            2.0 * jnp.sum(jnp.log(jnp.diagonal(lower_factor))),
            0.0,
        )
        rows_of_panel = from_root(rows_solved, "tile", elimination_round)
        boundary_column = (elimination_round + 1) * rows_of_block
        coupling_transposed = lax.dynamic_slice_in_dim(rows_of_panel, row_start, rows_of_block, 1)
        cleared_panel = trailing_matrix.at[
            :, elimination_round * rows_of_block : boundary_column
        ].set(0.0)
        updated_block = cleared_panel - jnp.dot(
            coupling_transposed.T, rows_of_panel, precision=precise
        )
        trailing_matrix = jnp.where(
            index_of_tile > elimination_round, updated_block, trailing_matrix
        )
        local_columns = jnp.where(index_of_tile <= elimination_round, coupling_transposed, 0.0)
        schur_rows = schur_rows.at[:, :boundary_column].add(
            jnp.dot(local_columns.T, rows_of_panel[:, :boundary_column], precision=precise)
        )
    log_all = lax.psum(log_total, "tile")
    interior_logdet = (log_all / node_count).reshape(1)
    incoming = from_behind(rho[0] * rho[0] * schur_rows, "tm", -1)
    separator_block = separator - rho[1] * rho[1] * schur_rows - incoming
    separator_coupling = -(rho[0] * rho[1]) * schur_rows
    return (separator_block[None], separator_coupling[None], interior_logdet)


def solution(mesh):
    in_specs = (
        P("tile", None),
        P(),
        P("tm"),
        P("tm"),
        P("tile", "tm", None, None),
        P("tile", "tm", None),
        P("tile", "tm", None),
    )
    out_specs = (P("tm", "tile", None), P("tm", "tile", None), P("tm"))
    return jax.shard_map(
        on_device, mesh=mesh, in_specs=in_specs, out_specs=out_specs, check_vma=False
    )
```

profile of v0, /device:TPU:6, one launch (start us, length us, event | category | flops | bytes accessed | tf_op | source)
XLA Modules:
  0.0 866.4 jit_solution(16232243364049365232)
XLA Ops:
  9.9 7.3 all-to-all-start.1
  18.5 5.0 scatter_fusion
  23.6 6.9 all-to-all-start
  30.5 6.1 copy.59
  37.9 7.9 broadcast_multiply_fusion.2
  45.8 18.4 %all-to-all-done = f32[16,2,16,768]{3,2,1,0:T(8,128)S(1)} async-done(((f32[16,2,16,768]{3,2,1,0:T(8,128)}), f32[16,2,16,768]{3,2,1,0:T(8,128)S(1)}, u32[]{:S(2)}, u32[]{:S(2)}) %all-to-all-start) | async-done | bytes 1572896 | tf_op jit(solution)/shard_map/all_to_all | solution.py:47
  64.2 4.5 fusion.49
  68.8 3.8 fusion.30
  78.4 4.7 fusion.24
  88.7 11.7 %cholesky.453 = f32[128,128]{1,0:T(8,128)S(1)} custom-call(f32[128,128]{1,0:T(8,128)S(1)} %cholesky.669), custom_call_target="Cholesky" | custom-call | tf_op jit(solution)/shard_map/jit(cholesky)/cholesky | solution.py:66
  100.4 9.8 %custom-call.45 = f32[1,128,128]{1,2,0:T(8,128)S(1)} custom-call(f32[1,128,128]{2,1,0:T(8,128)S(1)} %get-tuple-element.139), custom_call_target="InvertDiagBlocksLowerTriangular" | custom-call | tf_op jit(solution)/shard_map/jit(cholesky)/cholesky | solution.py:66
  113.2 11.7 %cholesky.472 = f32[128,128]{1,0:T(8,128)S(1)} custom-call(f32[128,128]{1,0:T(8,128)S(1)} %cholesky.673), custom_call_target="Cholesky" | custom-call | tf_op jit(solution)/shard_map/jit(cholesky)/cholesky | solution.py:66
  125.0 10.2 %custom-call.46 = f32[1,128,128]{1,2,0:T(8,128)S(1)} custom-call(f32[1,128,128]{2,1,0:T(8,128)S(1)} %get-tuple-element.136), custom_call_target="InvertDiagBlocksLowerTriangular" | custom-call | tf_op jit(solution)/shard_map/jit(cholesky)/cholesky | solution.py:66
  137.1 11.7 %cholesky.493 = f32[128,128]{1,0:T(8,128)S(1)} custom-call(f32[128,128]{1,0:T(8,128)S(1)} %cholesky.678), custom_call_target="Cholesky" | custom-call | tf_op jit(solution)/shard_map/jit(cholesky)/cholesky | solution.py:66
  149.5 9.8 %custom-call.47 = f32[1,128,128]{1,2,0:T(8,128)S(1)} custom-call(f32[1,128,128]{2,1,0:T(8,128)S(1)} %get-tuple-element.133), custom_call_target="InvertDiagBlocksLowerTriangular" | custom-call | tf_op jit(solution)/shard_map/jit(cholesky)/cholesky | solution.py:66
  161.2 11.9 %cholesky.512 = f32[128,128]{1,0:T(8,128)S(1)} custom-call(f32[128,128]{1,0:T(8,128)S(1)} %cholesky.683), custom_call_target="Cholesky" | custom-call | tf_op jit(solution)/shard_map/jit(cholesky)/cholesky | solution.py:66
  173.8 9.8 %custom-call.48 = f32[1,128,128]{1,2,0:T(8,128)S(1)} custom-call(f32[1,128,128]{2,1,0:T(8,128)S(1)} %get-tuple-element.130), custom_call_target="InvertDiagBlocksLowerTriangular" | custom-call | tf_op jit(solution)/shard_map/jit(cholesky)/cholesky | solution.py:66
  185.4 11.7 %cholesky.531 = f32[128,128]{1,0:T(8,128)S(1)} custom-call(f32[128,128]{1,0:T(8,128)S(1)} %cholesky.688), custom_call_target="Cholesky" | custom-call | tf_op jit(solution)/shard_map/jit(cholesky)/cholesky | solution.py:66
  197.8 9.8 %custom-call.49 = f32[1,128,128]{1,2,0:T(8,128)S(1)} custom-call(f32[1,128,128]{2,1,0:T(8,128)S(1)} %get-tuple-element.127), custom_call_target="InvertDiagBlocksLowerTriangular" | custom-call | tf_op jit(solution)/shard_map/jit(cholesky)/cholesky | solution.py:66
  209.1 12.1 %cholesky.548 = f32[128,128]{1,0:T(8,128)S(1)} custom-call(f32[128,128]{1,0:T(8,128)S(1)} %convolution_subtract_fusion.17), custom_call_target="Cholesky" | custom-call | tf_op jit(solution)/shard_map/jit(cholesky)/cholesky | solution.py:66
  228.9 17.3 %while.8 = (s32[]{:T(128)}, f32[768,768]{1,0:T(8,128)}, s32[6,2]{0,1:T(2,128)S(1)}, f32[6,128,128]{2,1,0:T(8,128)S(1)}, s32[]{:T(128)}) while((s32[]{:T(128)}, f32[768,768]{1,0:T(8,128)}, s32[6,2]{0,1:T(2,128)S(1)}, f32[6,128,128]{2,1,0:T(8,128)S(1)}, s32[]{:T(128)}) %tuple.100), condition=%wide.while_cond.3, body=%wide.while_body.3.sunk | while | flops 2 | bytes 131189 | solution.py:68
  246.2 59.0 %custom-call.50 = f32[6,128,128]{1,2,0:T(8,128)S(1)} custom-call(f32[6,128,128]{2,1,0:T(8,128)S(1)} %get-tuple-element.63), custom_call_target="InvertDiagBlocksLowerTriangular" | custom-call | tf_op jit(solution)/shard_map/triangular_solve/custom-call.5 | solution.py:68
  306.8 2.9 constant_dynamic-update-slice_fusion.4
  309.9 2.6 convolution_subtract_fusion.7
  315.4 3.8 convolution_subtract_fusion.1
  322.2 5.3 convolution_subtract_fusion.6
  330.2 7.4 fusion.19
  339.0 3.2 constant_dynamic-update-slice_fusion
  342.2 10.1 %convolution_subtract_fusion.5 = f32[128,1536]{0,1:T(8,128)} fusion(f32[640,1536]{1,0:T(8,128)} %get-tuple-element.154, f32[768,1536]{0,1:T(8,128)} %select_dynamic-update-slice_fusion.1, f32[768,768]{1,0:T(8,128)} %get-tuple-element.265), kind=kOutput, calls=%fused_computation.37 | convolution fusion | flops 1510146048 | bytes 5832704 | tf_op jit(solution)/shard_map/triangular_solve/dot.20 | solution.py:68
  359.5 30.6 %all-reduce.5.cloned.1.call-done = f32[768,1536]{0,1:T(8,128)} async-done(((f32[768,1536]{0,1:T(8,128)}), f32[768,1536]{0,1:T(8,128)}) %all-reduce.5.cloned.1.call-update) | async-done | bytes 4718608 | tf_op jit(solution)/shard_map/psum | solution.py:9
  390.1 17.4 %subtract_select_fusion = f32[768,1536]{0,1:T(8,128)} fusion(f32[768,1536]{0,1:T(8,128)} %copy-done.1, f32[768,1536]{0,1:T(8,128)} %get-tuple-element.106, f32[768,1536]{0,1:T(8,128)} %all-reduce.5.cloned.1.call-done, pred[]{:T(512)S(6)} %gt.3, s32[]{:T(128)S(6)} %select_n.76), kind=kOutput, calls=%fused_computation.10 | convolution fusion | flops 10873995264 | bytes 21233668 | tf_op jit(solution)/shard_map/dot_general | solution.py:80
  407.5 3.4 constant_dynamic-slice_fusion.2
  416.3 11.7 %cholesky.563 = f32[128,128]{1,0:T(8,128)S(1)} custom-call(f32[128,128]{1,0:T(8,128)S(1)} %cholesky.692), custom_call_target="Cholesky" | custom-call | tf_op jit(solution)/shard_map/jit(cholesky)/cholesky | solution.py:66
  428.8 9.8 %custom-call.51 = f32[1,128,128]{1,2,0:T(8,128)S(1)} custom-call(f32[1,128,128]{2,1,0:T(8,128)S(1)} %get-tuple-element.123), custom_call_target="InvertDiagBlocksLowerTriangular" | custom-call | tf_op jit(solution)/shard_map/jit(cholesky)/cholesky | solution.py:66
  441.6 11.7 %cholesky.582 = f32[128,128]{1,0:T(8,128)S(1)} custom-call(f32[128,128]{1,0:T(8,128)S(1)} %cholesky.696), custom_call_target="Cholesky" | custom-call | tf_op jit(solution)/shard_map/jit(cholesky)/cholesky | solution.py:66
  454.0 10.0 %custom-call.52 = f32[1,128,128]{1,2,0:T(8,128)S(1)} custom-call(f32[1,128,128]{2,1,0:T(8,128)S(1)} %get-tuple-element.120), custom_call_target="InvertDiagBlocksLowerTriangular" | custom-call | tf_op jit(solution)/shard_map/jit(cholesky)/cholesky | solution.py:66
  465.9 11.7 %cholesky.603 = f32[128,128]{1,0:T(8,128)S(1)} custom-call(f32[128,128]{1,0:T(8,128)S(1)} %cholesky.701), custom_call_target="Cholesky" | custom-call | tf_op jit(solution)/shard_map/jit(cholesky)/cholesky | solution.py:66
  478.3 9.8 %custom-call.53 = f32[1,128,128]{1,2,0:T(8,128)S(1)} custom-call(f32[1,128,128]{2,1,0:T(8,128)S(1)} %get-tuple-element.117), custom_call_target="InvertDiagBlocksLowerTriangular" | custom-call | tf_op jit(solution)/shard_map/jit(cholesky)/cholesky | solution.py:66
  490.0 12.1 %cholesky.622 = f32[128,128]{1,0:T(8,128)S(1)} custom-call(f32[128,128]{1,0:T(8,128)S(1)} %cholesky.706), custom_call_target="Cholesky" | custom-call | tf_op jit(solution)/shard_map/jit(cholesky)/cholesky | solution.py:66
  502.8 9.8 %custom-call.54 = f32[1,128,128]{1,2,0:T(8,128)S(1)} custom-call(f32[1,128,128]{2,1,0:T(8,128)S(1)} %get-tuple-element.114), custom_call_target="InvertDiagBlocksLowerTriangular" | custom-call | tf_op jit(solution)/shard_map/jit(cholesky)/cholesky | solution.py:66
  514.3 11.7 %cholesky.641 = f32[128,128]{1,0:T(8,128)S(1)} custom-call(f32[128,128]{1,0:T(8,128)S(1)} %cholesky.711), custom_call_target="Cholesky" | custom-call | tf_op jit(solution)/shard_map/jit(cholesky)/cholesky | solution.py:66
  526.8 9.8 %custom-call.55 = f32[1,128,128]{1,2,0:T(8,128)S(1)} custom-call(f32[1,128,128]{2,1,0:T(8,128)S(1)} %get-tuple-element.111), custom_call_target="InvertDiagBlocksLowerTriangular" | custom-call | tf_op jit(solution)/shard_map/jit(cholesky)/cholesky | solution.py:66
  538.1 11.9 %cholesky.658 = f32[128,128]{1,0:T(8,128)S(1)} custom-call(f32[128,128]{1,0:T(8,128)S(1)} %convolution_subtract_fusion.16), custom_call_target="Cholesky" | custom-call | tf_op jit(solution)/shard_map/jit(cholesky)/cholesky | solution.py:66
  554.5 2.6 fusion.43
  557.1 17.1 %while.9 = (s32[]{:T(128)}, f32[768,768]{1,0:T(8,128)}, s32[6,2]{0,1:T(2,128)S(1)}, f32[6,128,128]{2,1,0:T(8,128)S(1)}, s32[]{:T(128)}) while((s32[]{:T(128)}, f32[768,768]{1,0:T(8,128)}, s32[6,2]{0,1:T(2,128)S(1)}, f32[6,128,128]{2,1,0:T(8,128)S(1)}, s32[]{:T(128)}) %tuple.110), condition=%wide.while_cond.3.clone, body=%wide.while_body.3.clone.sunk | while | flops 2 | bytes 131189 | solution.py:68
  574.2 59.0 %custom-call.56 = f32[6,128,128]{1,2,0:T(8,128)S(1)} custom-call(f32[6,128,128]{2,1,0:T(8,128)S(1)} %get-tuple-element.64), custom_call_target="InvertDiagBlocksLowerTriangular" | custom-call | tf_op jit(solution)/shard_map/triangular_solve/custom-call.5 | solution.py:68
  633.1 2.9 constant_dynamic-update-slice_fusion.14
  636.3 2.6 convolution_subtract_fusion.4
  641.8 3.8 convolution_subtract_fusion
  648.6 5.3 convolution_subtract_fusion.3
  656.6 7.6 fusion.16
  665.6 3.2 constant_dynamic-update-slice_fusion.10
  668.8 9.6 %convolution_subtract_fusion.2 = f32[128,1536]{0,1:T(8,128)} fusion(f32[640,1536]{1,0:T(8,128)} %get-tuple-element.166, f32[768,1536]{0,1:T(8,128)} %get-tuple-element.105, f32[768,768]{1,0:T(8,128)} %get-tuple-element.266), kind=kOutput, calls=%fused_computation.34 | convolution fusion | flops 1510146048 | bytes 5832704 | tf_op jit(solution)/shard_map/triangular_solve/dot.20 | solution.py:68
  689.4 8.7 %fusion.54 = f32[768,768]{0,1:T(8,128)S(1)} fusion(f32[768,1536]{0,1:T(8,128)} %all-reduce.5.cloned.1.call-done, s32[]{:T(128)S(6)} %select_n.76, pred[]{:T(512)S(6)} %le.6, pred[]{:T(512)} %compare_reduce_fusion.12), kind=kOutput, calls=%fused_computation.85 | convolution fusion | flops 5436997632 | bytes 7077894 | tf_op jit(solution)/shard_map/dot_general | solution.py:88
  698.2 17.7 %all-reduce.7.cloned.1.call-done = f32[768,1536]{0,1:T(8,128)} async-done(((f32[768,1536]{0,1:T(8,128)}), f32[768,1536]{0,1:T(8,128)}) %all-reduce.7.cloned.1.call-update) | async-done | bytes 4718608 | tf_op jit(solution)/shard_map/psum | solution.py:9
  715.9 15.3 %pad_add_fusion = f32[768,1536]{0,1:T(8,128)S(1)} fusion(f32[768,768]{0,1:T(8,128)S(1)} %fusion.54, f32[768,1536]{0,1:T(8,128)} %all-reduce.7.cloned.1.call-done, s32[]{:T(128)S(6)} %select_n.76, pred[]{:T(512)S(6)} %le.7), kind=kOutput, calls=%fused_computation.11 | convolution fusion | flops 10873405440 | bytes 14155781 | tf_op jit(solution)/shard_map/dot_general | solution.py:88
  731.3 4.3 multiply_bitcast_fusion
  739.0 6.3 gather_fusion
  746.6 12.3 %gather_fusion.1 = f32[768]{0:T(1024)S(1)} fusion(f32[768,768]{1,0:T(8,128)} %get-tuple-element.91, s32[768]{0:T(1024)S(1)} %or_reduce_fusion), kind=kCustom, calls=%fused_computation.1 | custom fusion | bytes 12288 | tf_op jit(solution)/shard_map/jit(diagonal)/cond/branch_0_fun/gather | solution.py:71
  761.4 3.0 psum.23
  765.0 6.0 copy.94
  771.1 72.9 %collective-permute-done = f32[768,1536]{0,1:T(8,128)} collective-permute-done((f32[768,1536]{0,1:T(8,128)}, f32[768,1536]{0,1:T(8,128)}, u32[]{:S(2)}, u32[]{:S(2)}) %collective-permute-start) | collective-permute-done | bytes 4718624 | tf_op jit(solution)/shard_map/ppermute | solution.py:15
  843.9 8.2 subtract_bitcast_fusion
  852.1 6.0 copy.93
  (190 shorter events, 128.9 us)
Async XLA Ops:
  7.2 11.4 %copy-start.16 = (f32[1,32,16,768]{3,2,1,0:T(8,128)S(1)}, f32[1,32,16,768]{3,2,1,0:T(8,128)}, u32[]{:S(2)}) copy-start(f32[1,32,16,768]{3,2,1,0:T(8,128)} %param.22) | copy-start | bytes 4718596
  9.9 13.6 %all-to-all-start.1 = ((f32[16,2,16]{2,1,0:T(2,128)}), f32[16,2,16]{2,1,0:T(2,128)S(1)}, u32[]{:S(2)}, u32[]{:S(2)}) async-start(f32[16,2,16]{2,1,0:T(2,128)} %bitcast.6), calls=%async_computation.1 | async-start | bytes 32768 | tf_op jit(solution)/shard_map/all_to_all | solution.py:48
  23.6 40.6 %all-to-all-start = ((f32[16,2,16,768]{3,2,1,0:T(8,128)}), f32[16,2,16,768]{3,2,1,0:T(8,128)S(1)}, u32[]{:S(2)}, u32[]{:S(2)}) async-start(f32[16,2,16,768]{3,2,1,0:T(8,128)} %bitcast.4), calls=%async_computation | async-start | bytes 3145728 | tf_op jit(solution)/shard_map/all_to_all | solution.py:47
  30.5 359.6 %all-reduce.5.cloned.1.call-start = ((), (), s32[]{:S(2)}) async-start(), calls=%async_computation.2 | async-start | bytes 9437184 | tf_op jit(solution)/shard_map/psum | solution.py:9
  30.5 6.1 copy-start.17
  30.5 6.8 copy-start.18
  64.2 4.5 copy-start
  72.6 3.6 copy-start.1
  87.3 1.4 copy-start.5
  329.3 0.9 copy-start.12
  352.3 2.5 copy-start.6
  352.3 2.6 copy-start.8
  354.7 1.1 copy-start.10
  354.8 1.3 copy-start.14
  359.4 356.5 %all-reduce.7.cloned.1.call-start = ((), (), s32[]{:S(2)}) async-start(), calls=%async_computation.3 | async-start | bytes 9437184 | tf_op jit(solution)/shard_map/psum | solution.py:9
  414.9 1.4 copy-start.4
  655.6 0.9 copy-start.13
  678.4 2.6 copy-start.7
  678.4 2.7 copy-start.9
  681.0 1.1 copy-start.11
  681.1 1.3 copy-start.15
  685.7 0.7 copy-start.19
  731.2 5.3 copy-start.2
  731.3 7.7 copy-start.3
  736.5 107.4 %collective-permute-start = (f32[768,1536]{0,1:T(8,128)}, f32[768,1536]{0,1:T(8,128)}, u32[]{:S(2)}, u32[]{:S(2)}) collective-permute-start(f32[768,1536]{0,1:T(8,128)} %get-tuple-element.99), channel_id=1, source_target_pairs={{2,0},{4,2},{6,4},{8,6},{10,8},{12,10},{14,12},{16,14},{18,16},{20... | collective-permute-start | bytes 14155784 | tf_op jit(solution)/shard_map/ppermute | solution.py:15
Sparse Core Ops, SparseCore 0:
  359.6 30.4 all-reduce.4
  685.8 30.0 all-reduce.6
where the time goes:
time: 875 us; the launch traced here: 866 us
  other arithmetic  417 us (48%)
  matrix products  148 us (17%)
  waiting for transfers between devices  140 us (16%)
  local copies, waits for them, and re-layouts  113 us (13%)
  between operations  29.5 us (3%)
  starting transfers between devices  16.7 us (2%)
    another operation x45, other arithmetic, on_device(): lower_factor = jnp.linalg.cholesky(diag_tile)  248 us
    another operation x5, other arithmetic, on_device(): lax.linalg.triangular_solve(lower_factor, seeded, left_side=True, lower=T...  123 us
    another operation x22, matrix products, on_device(): lax.linalg.triangular_solve(lower_factor, seeded, left_side=True, lower=T...  82.4 us
    ppermute x1, waiting for transfers between devices, from_behind(): return lax.ppermute(block, axis, route)  72.9 us
    psum x2, waiting for transfers between devices, from_root(): return lax.psum(kept, axis)  48.3 us
    another operation x49, local copies, waits for them, and re-layouts, on_device(): lax.linalg.triangular_solve(lower_factor, seeded, left_side=True, lower=T...  47.1 us
    unnamed x55, local copies, waits for them, and re-layouts  33.1 us
    dot_general x2, matrix products, on_device(): jnp.dot(local_columns.T, rows_of_panel[:, :boundary_column], precision=pr...  24.1 us
  transfers between devices with their start and end apart: 5, of which 4 were waited for; matrix products, arithmetic and copies ran while one was open for 7% of the time, Pallas kernels for 0%

commit v1 on v0

v1 whole, which is shorter than its diff:
```python
import functools
import jax
import jax.numpy as jnp
from jax import lax
from jax.experimental import pallas as pl
from jax.experimental.pallas import tpu as pltpu
from jax.sharding import PartitionSpec as P

def halves(x):
    high = x.astype(jnp.bfloat16)
    return high, (x - high.astype(jnp.float32)).astype(jnp.bfloat16)

def dot3(a, b):
    ah, al = halves(a); bh, bl = halves(b)
    return jnp.dot(jnp.concatenate([ah, al, ah], 1), jnp.concatenate([bh, bh, bl], 0), preferred_element_type=jnp.float32)

def pair_inverse(a, b, d):
    det = a * d - b * b
    r = 1.0 / det
    return d * r, -b * r, a * r, det

def invert_tile(tiles, log_det):
    width = tiles[0].shape[1]
    shape = (8, width)
    lane = lax.broadcasted_iota(jnp.int32, shape, 1)
    sub = lax.broadcasted_iota(jnp.int32, shape, 0)
    for p in range(0, width, 4):
        home, first = p // 8, p % 8
        cols = [[jnp.broadcast_to(t[:, p + j:p + j + 1], shape) for t in tiles] for j in range(4)]
        s = {}
        for j in range(4):
            for i in range(j, 4):
                s[i, j] = jnp.broadcast_to(cols[j][home][first + i:first + i + 1, :], shape)
        a, b, d, det1 = pair_inverse(s[0, 0], s[1, 0], s[1, 1])
        q = [[s[2, 0], s[2, 1]], [s[3, 0], s[3, 1]]]
        m = [[q[i][0] * a + q[i][1] * b, q[i][0] * b + q[i][1] * d] for i in range(2)]
        u = s[2, 2] - (m[0][0] * q[0][0] + m[0][1] * q[0][1])
        v = s[3, 2] - (m[1][0] * q[0][0] + m[1][1] * q[0][1])
        w = s[3, 3] - (m[1][0] * q[1][0] + m[1][1] * q[1][1])
        u, v, w, det2 = pair_inverse(u, v, w)
        log_det = log_det + (jnp.log(det1) + jnp.log(det2))
        lower = [[u * m[0][j] + v * m[1][j] for j in range(2)], [v * m[0][j] + w * m[1][j] for j in range(2)]]
        w00 = a + (m[0][0] * lower[0][0] + m[1][0] * lower[1][0])
        w01 = b + (m[0][0] * lower[0][1] + m[1][0] * lower[1][1])
        w11 = d + (m[0][1] * lower[0][1] + m[1][1] * lower[1][1])
        inv = [[w00, w01, -lower[0][0], -lower[1][0]],
               [w01, w11, -lower[0][1], -lower[1][1]],
               [-lower[0][0], -lower[0][1], u, v],
               [-lower[1][0], -lower[1][1], v, w]]
        here = (lane >= p) & (lane < p + 4)
        rows = []
        for i in range(4):
            row = jnp.broadcast_to(tiles[home][first + i:first + i + 1, :], shape)
            rows.append(jnp.where(here, jnp.where(lane == p + i, 1.0, 0.0), row))
        out = [(inv[i][0] * rows[0] + inv[i][1] * rows[1]) + (inv[i][2] * rows[2] + inv[i][3] * rows[3]) for i in range(4)]
        new = []
        for t, tile in enumerate(tiles):
            kept = jnp.where(here, 0.0, tile)
            kept = kept - ((cols[0][t] * out[0] + cols[1][t] * out[1]) + (cols[2][t] * out[2] + cols[3][t] * out[3]))
            if t == home:
                for i in range(4):
                    kept = jnp.where(sub == first + i, out[i], kept)
            new.append(kept)
        tiles = new
    return tiles, log_det

def invert_body(x_ref, ld_ref, col_ref, row_ref, tile):
    n = x_ref.shape[0]
    ld_ref[...] = jnp.zeros_like(ld_ref)
    def step(k, _):
        at = pl.ds(pl.multiple_of(k * tile, tile), tile)
        tiles = [x_ref[pl.ds(pl.multiple_of(k * tile + 8 * t, 8), 8), at] for t in range(tile // 8)]
        tiles, ld = invert_tile(tiles, ld_ref[...])
        ld_ref[...] = ld
        w = jnp.concatenate(tiles, 0)
        col_ref[...] = x_ref[:, at]
        x_ref[:, at] = jnp.zeros((n, tile), jnp.float32)
        row = dot3(w, x_ref[at, :])
        row_ref[...] = row
        row_ref[:, at] = w
        row = row_ref[...]
        bh, bl = halves(row)
        right = jnp.concatenate([bh, bh, bl], 0)
        for i in range(n // tile):
            rows = slice(i * tile, (i + 1) * tile)
            ah, al = halves(col_ref[rows, :])
            x_ref[rows, :] -= jnp.dot(jnp.concatenate([ah, al, ah], 1), right, preferred_element_type=jnp.float32)
        x_ref[at, :] = row
        return 0
    lax.fori_loop(0, n // tile, step, 0)

def invert_kernel(a_ref, x_ref, ld_ref, col_ref, row_ref, *, tile):
    x_ref[...] = a_ref[...]
    invert_body(x_ref, ld_ref, col_ref, row_ref, tile)

def spd_inverse(a, tile=128):
    n = a.shape[0]
    x, ld = pl.pallas_call(
        functools.partial(invert_kernel, tile=tile),
        out_shape=(jax.ShapeDtypeStruct((n, n), jnp.float32), jax.ShapeDtypeStruct((8, tile), jnp.float32)),
        in_specs=[pl.BlockSpec(memory_space=pltpu.VMEM)],
        out_specs=(pl.BlockSpec(memory_space=pltpu.VMEM),) * 2,
        scratch_shapes=[pltpu.VMEM((n, tile), jnp.float32), pltpu.VMEM((tile, n), jnp.float32)],
        compiler_params=pltpu.CompilerParams(vmem_limit_bytes=40 << 20),
    )(a)
    return x, ld[0, 0]


def order_kernel(step_ref, value_ref, weight_ref, out_ref):
    for k in range(value_ref.shape[0]):
        out_ref[step_ref[k]] = value_ref[k] * jnp.sqrt(weight_ref[k])


def by_step(values, weights, steps):
    return pl.pallas_call(
        order_kernel,
        out_shape=jax.ShapeDtypeStruct(values.shape, jnp.float32),
        in_specs=[
            pl.BlockSpec(memory_space=pltpu.SMEM),
            pl.BlockSpec(memory_space=pltpu.VMEM),
            pl.BlockSpec(memory_space=pltpu.VMEM),
        ],
        out_specs=pl.BlockSpec(memory_space=pltpu.VMEM),
        compiler_params=pltpu.CompilerParams(vmem_limit_bytes=40 << 20),
    )(steps, values, weights[..., None])


def matmul(a, b, contract):
    return lax.dot_general(a, b, (contract, ((), ())), precision=lax.Precision.HIGH)


def scaled_inverse(a):
    scale = lax.rsqrt(jnp.diagonal(a))
    inverse, log_det = spd_inverse(a * scale[:, None] * scale[None, :])
    return inverse, scale, log_det - 2.0 * jnp.sum(jnp.log(scale))


def from_behind(block, axis, distance):
    devices = range(lax.axis_size(axis))
    route = [(i - distance, i) for i in devices if i - distance in devices]
    return lax.ppermute(block, axis, route)


def on_device(prior_space, node_gain, time_diag, rho, obs_values, obs_weight, obs_step):
    size, node_count = prior_space.shape
    part_count = lax.axis_size("tm")
    index_of_tile = lax.axis_index("tile")
    first = index_of_tile == 0
    own_at = index_of_tile * size
    sent = by_step(obs_values[0], obs_weight[0], obs_step[0, 0])
    sent = sent.reshape(part_count, 2, sent.shape[1], size)
    rows = lax.all_to_all(sent, "tm", split_axis=0, concat_axis=0, tiled=True)
    halves_of = [rows[:, s].reshape(-1, size) for s in range(2)]
    prior_own = jnp.where(first, prior_space[:, :size], prior_space[:, size:])
    prior_other = jnp.where(first, prior_space[:, size:], prior_space[:, :size])
    gain_own = jnp.where(first, node_gain[:size], node_gain[size:])
    gain_other = jnp.where(first, node_gain[size:], node_gain[:size])
    diag = time_diag[0] * prior_own + matmul(halves_of[0], halves_of[0], ((0,), (0,)))
    cross = time_diag[0] * prior_other
    inverse, scale, log_first = scaled_inverse(diag)
    panel = scale[:, None] * matmul(inverse, scale[:, None] * cross, ((1,), (0,)))
    swap = [(0, 1), (1, 0)]
    panel_other = lax.ppermute(panel, "tile", swap)
    separator_own = time_diag[1] * prior_own + matmul(halves_of[1], halves_of[1], ((0,), (0,)))
    reduced = diag - matmul(cross, panel_other, ((1,), (0,)))
    inverse, scale, log_second = scaled_inverse(reduced)
    log_other = lax.ppermute(log_first.reshape(1), "tile", swap)
    interior_logdet = (log_second.reshape(1) + log_other) / node_count
    left = gain_own * scale
    schur_own = left[:, None] * inverse * left[None, :]
    schur_other = -left[:, None] * matmul(inverse, scale[:, None] * panel_other.T, ((1,), (0,))) * gain_other[None, :]
    schur_rows = jnp.where(
        first,
        jnp.concatenate([schur_own, schur_other], 1),
        jnp.concatenate([schur_other, schur_own], 1),
    )
    incoming = from_behind(rho[0] * rho[0] * schur_rows, "tm", -1)
    gram = jnp.where(
        first,
        jnp.concatenate([separator_own, time_diag[1] * prior_other], 1),
        jnp.concatenate([time_diag[1] * prior_other, separator_own], 1),
    )
    separator_block = gram - rho[1] * rho[1] * schur_rows - incoming
    separator_coupling = -(rho[0] * rho[1]) * schur_rows
    return (separator_block[None], separator_coupling[None], interior_logdet)


def solution(mesh):
    in_specs = (
        P("tile", None),
        P(),
        P("tm"),
        P("tm"),
        P("tile", "tm", None, None),
        P("tile", "tm", None),
        P("tile", "tm", None),
    )
    out_specs = (P("tm", "tile", None), P("tm", "tile", None), P("tm"))
    return jax.shard_map(
        on_device, mesh=mesh, in_specs=in_specs, out_specs=out_specs, check_vma=False
    )
```

time: 875 us -> 321 us (0.37)
  other arithmetic: 417 us -> 19.9 us
  matrix products: 148 us -> 23.5 us
  Pallas kernels: 0 us -> 106 us
  local copies, waits for them, and re-layouts: 113 us -> 30.4 us
  waiting for transfers between devices: 140 us -> 118 us
  between operations: 29.5 us -> 8.73 us
    another operation x51 -> x0, other arithmetic: 372 us -> none  [the longest x45 248 us: on_device(): lower_factor = jnp.linalg.cholesky(diag_tile)]
    pallas_call x0 -> x3, Pallas kernels: none -> 106 us  [the longest x2 104 us: spd_inverse(): pl.pallas_call(functools.partial(invert_kernel, tile=tile), out_shape=(ja...]
    another operation x42 -> x0, matrix products: 102 us -> none  [the longest x22 82.4 us: on_device(): lax.linalg.triangular_solve(lower_factor, seeded, left_side=True, lower=T...]
    psum x2 -> x0, waiting for transfers between devices: 48.3 us -> none  [from_root(): return lax.psum(kept, axis)]
    another operation x61 -> x1, local copies, waits for them, and re-layouts: 47.4 us -> 0.89 us  [by_step(): weights[..., None]]
    unnamed x55 -> x34, local copies, waits for them, and re-layouts: 33.1 us -> 8.52 us
    dot_general x4 -> x5, matrix products: 46 us -> 23.5 us  [matmul(): lax.dot_general(a, b, (contract, ((), ())), precision=lax.Precision.HIGH)]
    ppermute x1, waiting for transfers between devices: 72.9 us -> 87.1 us  [from_behind(): return lax.ppermute(block, axis, route)]
  transfers between devices with their start and end apart: 5 -> 4, of which waited for: 4 -> 3; matrix products, arithmetic and copies ran while one was open for 7% -> 5% of each run, Pallas kernels for 0% -> 0%
where the time goes in v1:
time: 321 us; the launch traced here: 318 us
  waiting for transfers between devices  118 us (37%)
  Pallas kernels  106 us (33%)
  local copies, waits for them, and re-layouts  30.4 us (9%)
  matrix products  23.5 us (7%)
  other arithmetic  19.9 us (6%)
  starting transfers between devices  11.5 us (4%)
  between operations  8.73 us (3%)
    pallas_call x2, Pallas kernels, spd_inverse(): pl.pallas_call(functools.partial(invert_kernel, tile=tile), out_shape=(ja...  104 us
    ppermute x1, waiting for transfers between devices, from_behind(): return lax.ppermute(block, axis, route)  87.1 us
    all_to_all x1, waiting for transfers between devices, on_device(): rows = lax.all_to_all(sent, 'tm', split_axis=0, concat_axis=0, tiled=True)  28.1 us
    dot_general x5, matrix products, matmul(): lax.dot_general(a, b, (contract, ((), ())), precision=lax.Precision.HIGH)  23.5 us
    gather x2, local copies, waits for them, and re-layouts, scaled_inverse(): scale = lax.rsqrt(jnp.diagonal(a))  18.7 us
    unnamed x34, local copies, waits for them, and re-layouts  8.52 us
    all_to_all x1, starting transfers between devices, on_device(): rows = lax.all_to_all(sent, 'tm', split_axis=0, concat_axis=0, tiled=True)  7.38 us
  transfers between devices with their start and end apart: 4, of which 3 were waited for; matrix products, arithmetic and copies ran while one was open for 5% of the time, Pallas kernels for 0%

profile of v1, /device:TPU:6, one launch (start us, length us, event | category | flops | bytes accessed | tf_op | source)
XLA Modules:
  0.0 318.2 jit_solution(10508368029581460980)
XLA Ops:
  0.6 0.9 copy.18.weight_ref
  1.5 0.0 copy-start
  1.5 1.4 copy-done
  2.9 0.0 copy-start.1
  2.9 0.7 copy-done.1
  3.6 1.9 shard_map.94
  5.5 0.0 copy-start.15
  5.5 7.4 %all-to-all-start = ((f32[16,2,16,768]{3,2,1,0:T(8,128)}), f32[16,2,16,768]{3,2,1,0:T(8,128)S(1)}, u32[]{:S(2)}, u32[]{:S(2)}) async-start(f32[16,2,16,768]{3,2,1,0:T(8,128)} %bitcast.4), calls=%async_computation | async-start | bytes 3145728 | tf_op jit(solution)/shard_map/all_to_all | solution.py:152
  12.9 0.0 copy-done.15
  12.9 0.6 fusion.26
  13.5 5.6 %broadcast_multiply_fusion = (f32[768,768]{1,0:T(8,128)}, f32[768,768]{1,0:T(8,128)}) fusion(f32[]{:T(128)} %bitcast, f32[768,1536]{1,0:T(8,128)} %param.7, pred[]{:T(512)S(6)} %eq.3), kind=kLoop, calls=%fused_computation.31 | loop fusion | flops 1179648 | bytes 9437189 | tf_op jit(solution)/shard_map/mul | solution.py:180
  19.1 28.1 %all-to-all-done = f32[16,2,16,768]{3,2,1,0:T(8,128)S(1)} async-done(((f32[16,2,16,768]{3,2,1,0:T(8,128)}), f32[16,2,16,768]{3,2,1,0:T(8,128)S(1)}, u32[]{:S(2)}, u32[]{:S(2)}) %all-to-all-start) | async-done | bytes 1572896 | tf_op jit(solution)/shard_map/all_to_all | solution.py:152
  47.2 0.0 copy-start.13
  47.2 1.2 copy-done.13
  48.4 4.9 %bitcast_add_fusion = f32[768,768]{1,0:T(8,128)S(1)} fusion(f32[]{:T(128)} %bitcast.8, f32[16,2,16,768]{3,2,1,0:T(8,128)} %copy-done.13, f32[768,1536]{1,0:T(8,128)} %param.7, pred[]{:T(512)S(6)} %eq.3), kind=kOutput, calls=%fused_computation.10 | convolution fusion | flops 907739136 | bytes 7864833 | tf_op jit(solution)/shard_map/dot_general | solution.py:129
  53.3 0.0 copy-start.4
  53.3 6.3 %gather_fusion = f32[768]{0:T(1024)S(1)} fusion(f32[768,768]{1,0:T(8,128)S(1)} %bitcast_add_fusion, s32[768]{0:T(1024)S(1)} %or_reduce_fusion), kind=kCustom, calls=%fused_computation | custom fusion | bytes 12288 | tf_op jit(solution)/shard_map/jit(diagonal)/cond/branch_0_fun/gather | solution.py:133
  59.6 0.6 multiply_reduce_fusion
  60.3 0.0 copy-done.4
  60.3 0.3 multiply_multiply_fusion.3.a_ref
  60.5 0.0 copy-start.8
  60.5 52.2 %shard_map.95 = (f32[768,768]{1,0:T(8,128)S(1)}, f32[8,128]{1,0:T(8,128)S(1)}) custom-call(f32[768,768]{1,0:T(8,128)S(1)} %multiply_multiply_fusion.3.a_ref), custom_call_target="tpu_custom_call" | custom-call | tf_op jit(solution)/shard_map/pallas_call | solution.py:98
  112.8 0.0 copy-done.8
  112.8 0.0 copy-start.16
  112.8 0.0 copy-start.5
  112.8 4.0 %fusion.12 = f32[768,768]{1,0:T(8,128)S(1)} fusion(f32[768,768]{1,0:T(8,128)S(1)} %get-tuple-element.7, f32[768,768]{1,0:T(8,128)S(1)} %copy-done.8, f32[768]{0:T(1024)S(1)} %get-tuple-element.19, f32[]{:T(128)} %bitcast.8), kind=kOutput, calls=%fused_computation.25 | convolution fusion | flops 2719678464 | bytes 7080964 | tf_op jit(solution)/shard_map/dot_general | solution.py:129
  116.8 0.1 collective-permute-start
  116.9 0.0 copy-done.16
  116.9 0.6 fusion.25
  118.8 2.7 collective-permute-done
  121.4 0.0 copy-start.10
  121.4 1.4 copy-done.10
  122.8 0.0 copy-done.5
  122.8 5.2 %fusion.15 = f32[768,768]{1,0:T(8,128)} fusion(f32[768,768]{1,0:T(8,128)S(1)} %copy-done.5, f32[768,768]{1,0:T(8,128)S(1)} %collective-permute-done, f32[768,768]{1,0:T(8,128)S(1)} %copy-done.8, f32[]{:T(128)} %bitcast.8), kind=kOutput, calls=%fused_computation.26 | convolution fusion | flops 2719088640 | bytes 9437188 | tf_op jit(solution)/shard_map/dot_general | solution.py:129
  128.0 0.0 copy-start.14
  128.0 12.4 %gather_fusion.1 = f32[768]{0:T(1024)S(1)} fusion(f32[768,768]{1,0:T(8,128)} %fusion.15, s32[768]{0:T(1024)S(1)} %or_reduce_fusion), kind=kCustom, calls=%fused_computation.1 | custom fusion | bytes 12288 | tf_op jit(solution)/shard_map/jit(diagonal)/cond/branch_0_fun/gather | solution.py:133
  140.5 0.0 copy-done.14
  140.5 0.7 fusion.24
  141.2 1.9 multiply_multiply_fusion.2.a_ref
  143.1 52.3 %shard_map.96 = (f32[768,768]{1,0:T(8,128)S(1)}, f32[8,128]{1,0:T(8,128)S(1)}) custom-call(f32[768,768]{1,0:T(8,128)S(1)} %multiply_multiply_fusion.2.a_ref), custom_call_target="tpu_custom_call" | custom-call | tf_op jit(solution)/shard_map/pallas_call | solution.py:98
  195.3 0.0 copy-start.11
  195.4 0.3 multiply_multiply_fusion.1
  195.6 0.0 copy-start.6
  195.6 2.2 copy-done.11
  197.9 3.1 multiply_multiply_fusion
  200.9 0.0 copy-start.2
  200.9 0.0 copy-done.6
  201.0 2.7 fusion.4
  203.7 0.2 copy-done.2
  203.8 3.0 collective-permute-start.1
  209.3 0.5 slice.58
  211.0 1.0 collective-permute-start.2
  212.0 6.3 %bitcast_add_fusion.1 = f32[768,768]{1,0:T(8,128)} fusion(f32[]{:T(128)} %bitcast, f32[16,2,16,768]{3,2,1,0:T(8,128)} %copy-done.13, f32[768,1536]{1,0:T(8,128)} %param.7, pred[]{:T(512)S(6)} %eq.3), kind=kOutput, calls=%fused_computation.11 | convolution fusion | flops 907739136 | bytes 7864833 | tf_op jit(solution)/shard_map/dot_general | solution.py:129
  218.3 0.5 slice.57
  220.1 0.0 collective-permute-done.2
  220.7 0.0 copy-start.3
  220.7 0.3 fusion.30
  221.0 1.4 copy-done.3
  222.4 2.7 fusion.3
  225.1 87.1 %collective-permute-done.1 = f32[768,1536]{1,0:T(8,128)} collective-permute-done((f32[768,1536]{1,0:T(8,128)}, f32[768,1536]{1,0:T(8,128)}, u32[]{:S(2)}, u32[]{:S(2)}) %collective-permute-start.1) | collective-permute-done | bytes 4718624 | tf_op jit(solution)/shard_map/ppermute | solution.py:141
  312.2 0.0 copy-done.7
  312.2 0.0 copy-done.9
  312.2 0.0 copy-done.12
  312.2 4.8 %fusion.2 = f32[1,768,1536]{2,1,0:T(8,128)} fusion(f32[768,1536]{1,0:T(8,128)} %collective-permute-done.1, f32[768,768]{1,0:T(8,128)S(1)} %copy-done.9, f32[768,768]{1,0:T(8,128)S(1)} %copy-done.12, f32[768,768]{1,0:T(8,128)S(1)} %copy-done.7, f32[768,768]{1,0:T(8,128)S(1)} %copy-done.3, f32[]{:T(128)} %bitcast.7, pred[]{:T(512)S(6)} %eq.3), kind=kLoop, calls=%fused_computation.5 | loop fusion | flops 10616832 | bytes 18874372 | tf_op jit(solution)/shard_map/broadcast_in_dim | solution.py:185
  (4 shorter events, 0.0 us)
Async XLA Ops:
  1.5 1.4 copy-start
  2.9 0.7 copy-start.1
  5.5 7.4 %copy-start.15 = (f32[2]{0:T(128)S(1)}, f32[2]{0:T(128)}, u32[]{:S(2)}) copy-start(f32[2]{0:T(128)} %param.9) | copy-start | bytes 28
  5.5 41.7 %all-to-all-start = ((f32[16,2,16,768]{3,2,1,0:T(8,128)}), f32[16,2,16,768]{3,2,1,0:T(8,128)S(1)}, u32[]{:S(2)}, u32[]{:S(2)}) async-start(f32[16,2,16,768]{3,2,1,0:T(8,128)} %bitcast.4), calls=%async_computation | async-start | bytes 3145728 | tf_op jit(solution)/shard_map/all_to_all | solution.py:152
  47.2 1.2 copy-start.13
  53.3 6.9 %copy-start.4 = (f32[768,768]{1,0:T(8,128)}, f32[768,768]{1,0:T(8,128)S(1)}, u32[]{:S(2)}) copy-start(f32[768,768]{1,0:T(8,128)S(1)} %bitcast_add_fusion) | copy-start | bytes 7077892
  60.5 52.2 %copy-start.8 = (f32[768,768]{1,0:T(8,128)S(1)}, f32[768,768]{1,0:T(8,128)}, u32[]{:S(2)}) copy-start(f32[768,768]{1,0:T(8,128)} %get-tuple-element.12) | copy-start | bytes 7077892
  112.8 4.1 %copy-start.16 = (f32[2]{0:T(128)S(1)}, f32[2]{0:T(128)}, u32[]{:S(2)}) copy-start(f32[2]{0:T(128)} %param.10) | copy-start | bytes 28
  112.8 10.1 %copy-start.5 = (f32[768,768]{1,0:T(8,128)S(1)}, f32[768,768]{1,0:T(8,128)}, u32[]{:S(2)}) copy-start(f32[768,768]{1,0:T(8,128)} %copy-done.4) | copy-start | bytes 7077892
  116.8 4.6 %collective-permute-start = (f32[768,768]{1,0:T(8,128)S(1)}, f32[768,768]{1,0:T(8,128)S(1)}, u32[]{:S(2)}, u32[]{:S(2)}) collective-permute-start(f32[768,768]{1,0:T(8,128)S(1)} %fusion.12), channel_id=1, source_target_pairs={{0,1},{1,0},{2,3},{3,2},{4,5},{5,4},{6,7},{7,6},{8,9},{9,8},{10,11... | collective-permute-start | bytes 7077896 | tf_op jit(solution)/shard_map/ppermute | solution.py:163
  121.4 1.4 copy-start.10
  128.0 12.4 %copy-start.14 = (f32[1536]{0:T(1024)S(1)}, f32[1536]{0:T(1024)}, u32[]{:S(2)}) copy-start(f32[1536]{0:T(1024)} %param.8) | copy-start | bytes 18436
  195.3 2.5 copy-start.11
  195.6 5.3 %copy-start.6 = (f32[768,768]{1,0:T(8,128)}, f32[768,768]{1,0:T(8,128)S(1)}, u32[]{:S(2)}) copy-start(f32[768,768]{1,0:T(8,128)S(1)} %multiply_multiply_fusion.1) | copy-start | bytes 7077892
  200.9 2.9 copy-start.2
  203.8 108.4 %collective-permute-start.1 = (f32[768,1536]{1,0:T(8,128)}, f32[768,1536]{1,0:T(8,128)}, u32[]{:S(2)}, u32[]{:S(2)}) collective-permute-start(f32[768,1536]{1,0:T(8,128)} %fusion.4), channel_id=1, source_target_pairs={{2,0},{4,2},{6,4},{8,6},{10,8},{12,10},{14,12},{16,14},{18,16},{20... | collective-permute-start | bytes 14155784 | tf_op jit(solution)/shard_map/ppermute | solution.py:141
  211.0 9.1 %collective-permute-start.2 = (f32[1]{0:T(128)}, f32[1]{0:T(128)}, u32[]{:S(2)}, u32[]{:S(2)}) collective-permute-start(f32[1]{0:T(128)} %bitcast.19), channel_id=1, source_target_pairs={{0,1},{1,0},{2,3},{3,2},{4,5},{5,4},{6,7},{7,6},{8,9},{9,8},{10,11... | collective-permute-start | bytes 20 | tf_op jit(solution)/shard_map/ppermute | solution.py:167
  220.7 1.7 copy-start.3
  222.4 89.9 %copy-start.7 = (f32[768,768]{1,0:T(8,128)S(1)}, f32[768,768]{1,0:T(8,128)}, u32[]{:S(2)}) copy-start(f32[768,768]{1,0:T(8,128)} %copy-done.6) | copy-start | bytes 7077892
  222.4 89.9 %copy-start.9 = (f32[768,768]{1,0:T(8,128)S(1)}, f32[768,768]{1,0:T(8,128)}, u32[]{:S(2)}) copy-start(f32[768,768]{1,0:T(8,128)} %get-tuple-element.11) | copy-start | bytes 7077892
  222.4 89.9 %copy-start.12 = (f32[768,768]{1,0:T(8,128)S(1)}, f32[768,768]{1,0:T(8,128)}, u32[]{:S(2)}) copy-start(f32[768,768]{1,0:T(8,128)} %bitcast_add_fusion.1) | copy-start | bytes 7077892

commit v2 on v1

--- a/solution.py
+++ b/solution.py
@@ -101,7 +101,8 @@
         in_specs=[pl.BlockSpec(memory_space=pltpu.VMEM)],
         out_specs=(pl.BlockSpec(memory_space=pltpu.VMEM),) * 2,
         scratch_shapes=[pltpu.VMEM((n, tile), jnp.float32), pltpu.VMEM((tile, n), jnp.float32)],
-        compiler_params=pltpu.CompilerParams(vmem_limit_bytes=40 << 20),
+        compiler_params=pltpu.CompilerParams(vmem_limit_bytes=24 << 20),
+        cost_estimate=pl.CostEstimate(flops=50 * n**3, bytes_accessed=8 * n * n, transcendentals=0),
     )(a)
     return x, ld[0, 0]
 
@@ -130,7 +131,8 @@
 
 
 def scaled_inverse(a):
-    scale = lax.rsqrt(jnp.diagonal(a))
+    here = jnp.eye(a.shape[0], dtype=jnp.bool_)
+    scale = lax.rsqrt(jnp.sum(jnp.where(here, a, 0.0), 1))
     inverse, log_det = spd_inverse(a * scale[:, None] * scale[None, :])
     return inverse, scale, log_det - 2.0 * jnp.sum(jnp.log(scale))
 
@@ -139,6 +141,30 @@
     devices = range(lax.axis_size(axis))
     route = [(i - distance, i) for i in devices if i - distance in devices]
     return lax.ppermute(block, axis, route)
+
+
+def pack(symmetric, tile=128):
+    count = symmetric.shape[0] // tile
+    rows = []
+    for r in range(count // 2):
+        low, high = (r + 1) * tile, (count - r) * tile
+        rows.append(
+            jnp.concatenate([symmetric[low - tile : low, :low], symmetric[high - tile : high, :high]], 1)
+        )
+    return jnp.concatenate(rows, 0)
+
+
+def unpack(packed, size, tile=128):
+    count = size // tile
+    rows = [None] * count
+    for r in range(count // 2):
+        low = (r + 1) * tile
+        line = packed[low - tile : low]
+        rows[r] = jnp.pad(line[:, :low], ((0, 0), (0, size - low)))
+        rows[count - 1 - r] = jnp.pad(line[:, low:], ((0, 0), (0, r * tile)))
+    lower = jnp.concatenate(rows, 0)
+    block = jnp.arange(size) // tile
+    return jnp.where(block[:, None] >= block[None, :], lower, lower.T)
 
 
 def on_device(prior_space, node_gain, time_diag, rho, obs_values, obs_weight, obs_step):
@@ -149,8 +175,10 @@
     own_at = index_of_tile * size
     sent = by_step(obs_values[0], obs_weight[0], obs_step[0, 0])
     sent = sent.reshape(part_count, 2, sent.shape[1], size)
-    rows = lax.all_to_all(sent, "tm", split_axis=0, concat_axis=0, tiled=True)
-    halves_of = [rows[:, s].reshape(-1, size) for s in range(2)]
+    halves_of = [
+        lax.all_to_all(sent[:, s], "tm", split_axis=0, concat_axis=0, tiled=True).reshape(-1, size)
+        for s in range(2)
+    ]
     prior_own = jnp.where(first, prior_space[:, :size], prior_space[:, size:])
     prior_other = jnp.where(first, prior_space[:, size:], prior_space[:, :size])
     gain_own = jnp.where(first, node_gain[:size], node_gain[size:])
@@ -169,17 +197,26 @@
     left = gain_own * scale
     schur_own = left[:, None] * inverse * left[None, :]
     schur_other = -left[:, None] * matmul(inverse, scale[:, None] * panel_other.T, ((1,), (0,))) * gain_other[None, :]
-    schur_rows = jnp.where(
+    decay = rho[0] * rho[0]
+    half = size // 2
+    own_next = unpack(from_behind(decay * pack(schur_own), "tm", -1), size)
+    sent_half = decay * jnp.where(first, schur_other[:half], schur_other[:, half:].T)
+    half_next = from_behind(sent_half, "tm", -1)
+    half_swapped = lax.ppermute(half_next, "tile", swap)
+    other_next = jnp.where(
         first,
-        jnp.concatenate([schur_own, schur_other], 1),
-        jnp.concatenate([schur_other, schur_own], 1),
+        jnp.concatenate([half_next, half_swapped], 0),
+        jnp.concatenate([half_swapped, half_next], 0).T,
     )
-    incoming = from_behind(rho[0] * rho[0] * schur_rows, "tm", -1)
-    gram = jnp.where(
-        first,
-        jnp.concatenate([separator_own, time_diag[1] * prior_other], 1),
-        jnp.concatenate([time_diag[1] * prior_other, separator_own], 1),
-    )
+
+    def in_order(own, other):
+        return jnp.where(
+            first, jnp.concatenate([own, other], 1), jnp.concatenate([other, own], 1)
+        )
+
+    schur_rows = in_order(schur_own, schur_other)
+    incoming = in_order(own_next, other_next)
+    gram = in_order(separator_own, time_diag[1] * prior_other)
     separator_block = gram - rho[1] * rho[1] * schur_rows - incoming
     separator_coupling = -(rho[0] * rho[1]) * schur_rows
     return (separator_block[None], separator_coupling[None], interior_logdet)

time: 321 us -> 270 us (0.84)
  waiting for transfers between devices: 118 us -> 50.5 us
  other arithmetic: 19.9 us -> 31.3 us
  starting transfers between devices: 11.5 us -> 20.1 us
  local copies, waits for them, and re-layouts: 30.4 us -> 25.4 us
  matrix products: 23.5 us -> 27.3 us
    ppermute x1 -> x2, waiting for transfers between devices: 87.1 us -> 37.2 us  [from_behind(): return lax.ppermute(block, axis, route)]
    gather x2 -> x0, local copies, waits for them, and re-layouts: 18.7 us -> none  [scaled_inverse(): scale = lax.rsqrt(jnp.diagonal(a))]
    all_to_all x1 -> x2, waiting for transfers between devices: 28.1 us -> 13.3 us  [on_device(): lax.all_to_all(sent[:, s], 'tm', split_axis=0, concat_axis=0, tiled=True)]
    concatenate x2 -> x5, other arithmetic: 0.29 us -> 14.4 us  [the longest x4 11.5 us: in_order(): jnp.concatenate([own, other], 1)]
    slice x1 -> x15, local copies, waits for them, and re-layouts: 0.58 us -> 10.6 us  [the longest x2 3.87 us: on_device(): schur_other[:half]]
    mul x1, other arithmetic: 2.74 us -> 9.93 us  [on_device(): separator_coupling = -(rho[0] * rho[1]) * schur_rows]
    all_to_all x1 -> x2, starting transfers between devices: 7.38 us -> 13.4 us  [on_device(): lax.all_to_all(sent[:, s], 'tm', split_axis=0, concat_axis=0, tiled=True)]
    concatenate x0 -> x3, local copies, waits for them, and re-layouts: none -> 5.06 us  [the longest x2 3.02 us: unpack(): lower = jnp.concatenate(rows, 0)]
  transfers between devices with their start and end apart: 4 -> 7, of which waited for: 3 -> 2; matrix products, arithmetic and copies ran while one was open for 5% -> 18% of each run, Pallas kernels for 0% -> 19%
where the time goes in v2:
time: 270 us; the launch traced here: 269 us
  Pallas kernels  105 us (39%)
  waiting for transfers between devices  50.5 us (19%)
  other arithmetic  31.3 us (12%)
  matrix products  27.3 us (10%)
  local copies, waits for them, and re-layouts  25.4 us (9%)
  starting transfers between devices  20.1 us (7%)
  between operations  8.96 us (3%)
    pallas_call x2, Pallas kernels, spd_inverse(): pl.pallas_call(functools.partial(invert_kernel, tile=tile), out_shape=(ja...  104 us
    ppermute x2, waiting for transfers between devices, from_behind(): return lax.ppermute(block, axis, route)  37.2 us
    dot_general x5, matrix products, matmul(): lax.dot_general(a, b, (contract, ((), ())), precision=lax.Precision.HIGH)  27.3 us
    all_to_all x2, starting transfers between devices, on_device(): lax.all_to_all(sent[:, s], 'tm', split_axis=0, concat_axis=0, tiled=True)  13.4 us
    all_to_all x2, waiting for transfers between devices, on_device(): lax.all_to_all(sent[:, s], 'tm', split_axis=0, concat_axis=0, tiled=True)  13.3 us
    concatenate x4, other arithmetic, in_order(): jnp.concatenate([own, other], 1)  11.5 us
    mul x1, other arithmetic, on_device(): separator_coupling = -(rho[0] * rho[1]) * schur_rows  9.93 us
    unnamed x29, local copies, waits for them, and re-layouts  5.97 us
  transfers between devices with their start and end apart: 7, of which 2 were waited for; matrix products, arithmetic and copies ran while one was open for 18% of the time, Pallas kernels for 19%

profile of v2, /device:TPU:6, one launch (start us, length us, event | category | flops | bytes accessed | tf_op | source)
XLA Modules:
  0.0 268.6 jit_solution(3891217829193336220)
XLA Ops:
  0.6 0.9 copy.20.weight_ref
  1.5 0.0 copy-start
  1.5 1.4 copy-done
  2.9 0.7 copy-done.1
  3.6 0.7 shard_map.94
  4.3 0.0 copy-start.10
  4.3 1.3 slice_bitcast_fusion.1
  5.6 7.3 %all-to-all-start.1 = ((f32[16,16,768]{2,1,0:T(8,128)}), f32[16,16,768]{2,1,0:T(8,128)S(1)}, u32[]{:S(2)}, u32[]{:S(2)}) async-start(f32[16,16,768]{2,1,0:T(8,128)} %get-tuple-element.17), calls=%async_computation.1 | async-start | bytes 1572864 | tf_op jit(solution)/shard_map/all_to_all | solution.py:179
  12.9 0.6 fusion.33
  13.5 4.6 %multiply_bitcast_fusion = (f32[1,768,768]{2,1,0:T(8,128)}, f32[768,768]{1,0:T(8,128)S(1)}) fusion(f32[]{:T(128)} %bitcast, f32[768,1536]{1,0:T(8,128)} %param.7, pred[]{:T(512)S(6)} %eq.9), kind=kLoop, calls=%fused_computation.26 | loop fusion | flops 1179648 | bytes 9437189 | tf_op jit(solution)/shard_map/concatenate | solution.py:214
  18.1 13.3 %all-to-all-done.1 = f32[16,16,768]{2,1,0:T(8,128)S(1)} async-done(((f32[16,16,768]{2,1,0:T(8,128)}), f32[16,16,768]{2,1,0:T(8,128)S(1)}, u32[]{:S(2)}, u32[]{:S(2)}) %all-to-all-start.1) | async-done | bytes 786464 | tf_op jit(solution)/shard_map/all_to_all | solution.py:179
  31.4 4.6 %select_reduce_fusion.1 = (f32[768]{0:T(1024)S(1)}, f32[768,768]{1,0:T(8,128)S(1)}) fusion(f32[16,16,768]{2,1,0:T(8,128)S(1)} %all-to-all-done.1, f32[768,1536]{1,0:T(8,128)} %param.7, pred[]{:T(512)S(6)} %eq.9, f32[]{:T(128)} %bitcast.10), kind=kOutput, calls=%fused_computation.24 | convolution fusion | flops 909507840 | bytes 8653829 | tf_op jit(solution)/shard_map/dot_general | solution.py:130
  36.0 0.0 copy-start.7
  36.0 0.8 multiply_reduce_fusion
  36.8 0.6 copy-done.7
  37.4 0.3 multiply_multiply_fusion.3.a_ref
  37.7 52.0 %shard_map.95 = (f32[768,768]{1,0:T(8,128)S(1)}, f32[8,128]{1,0:T(8,128)S(1)}) custom-call(f32[768,768]{1,0:T(8,128)S(1)} %multiply_multiply_fusion.3.a_ref), custom_call_target="tpu_custom_call" | custom-call | flops 22649241600 | bytes 4718592 | tf_op jit(solution)/shard_map/pallas_call | solution.py:98
  89.7 0.0 copy-start.11
  89.7 5.3 %fusion.14 = f32[768,768]{1,0:T(8,128)} fusion(f32[768,768]{1,0:T(8,128)S(1)} %get-tuple-element.7, f32[768,768]{1,0:T(8,128)S(1)} %get-tuple-element.14, f32[768]{0:T(1024)S(1)} %get-tuple-element.21, f32[]{:T(128)} %bitcast.10), kind=kOutput, calls=%fused_computation.32 | convolution fusion | flops 2719678464 | bytes 7080964 | tf_op jit(solution)/shard_map/dot_general | solution.py:130
  95.1 0.0 collective-permute-start
  95.1 6.2 %all-to-all-start = ((f32[16,16,768]{2,1,0:T(8,128)}), f32[16,16,768]{2,1,0:T(8,128)}, u32[]{:S(2)}, u32[]{:S(2)}) async-start(f32[16,16,768]{2,1,0:T(8,128)} %get-tuple-element.18), calls=%async_computation | async-start | bytes 1572864 | tf_op jit(solution)/shard_map/all_to_all | solution.py:179
  101.2 0.6 fusion.32
  103.0 0.0 copy-start.9
  103.0 0.0 collective-permute-done
  103.0 6.3 %select_reduce_fusion = (f32[768]{0:T(1024)S(1)}, f32[768,768]{1,0:T(8,128)S(1)}) fusion(f32[768,768]{1,0:T(8,128)} %copy-done.7, f32[768,768]{1,0:T(8,128)} %collective-permute-done, f32[768,768]{1,0:T(8,128)S(1)} %get-tuple-element.14, f32[]{:T(128)} %bitcast.10), kind=kOutput, calls=%fused_computation.20 | convolution fusion | flops 2720857344 | bytes 9440260 | tf_op jit(solution)/shard_map/dot_general | solution.py:130
  109.3 0.6 fusion.31
  109.9 0.3 multiply_multiply_fusion.2.a_ref
  110.1 52.3 %shard_map.96 = (f32[768,768]{1,0:T(8,128)S(1)}, f32[8,128]{1,0:T(8,128)S(1)}) custom-call(f32[768,768]{1,0:T(8,128)S(1)} %multiply_multiply_fusion.2.a_ref), custom_call_target="tpu_custom_call" | custom-call | flops 22649241600 | bytes 4718592 | tf_op jit(solution)/shard_map/pallas_call | solution.py:98
  162.4 0.3 multiply_multiply_fusion.1
  162.7 0.0 copy-start.8
  162.7 0.7 slice.125
  163.4 0.7 slice.127
  164.2 4.8 %multiply_multiply_fusion = f32[768,768]{1,0:T(8,128)S(1)} fusion(f32[768,768]{1,0:T(8,128)S(1)} %get-tuple-element.8, f32[768,768]{1,0:T(8,128)} %collective-permute-done, f32[768]{0:T(1024)S(1)} %get-tuple-element.19, f32[768]{0:T(1024)S(1)} %get-tuple-element.11, f32[768]{0:T(1024)S(1)} %get-tuple-element.23), kind=kOutput, calls=%fused_computation.15 | convolution fusion | flops 2719678464 | bytes 7087104 | tf_op jit(solution)/shard_map/dot_general | solution.py:130
  169.0 1.4 copy-done.2
  170.4 1.1 slice.137
  171.6 2.8 %copy.28 = f32[384,768]{0,1:T(8,128)} copy(f32[384,768]{1,0:T(8,128)} %slice.137) | data formatting | bytes 2359296 | tf_op jit(solution)/shard_map/slice | solution.py:203
  174.3 2.3 maximum_multiply_fusion
  176.6 2.5 collective-permute-start.1
  179.1 2.5 fusion.23
  181.6 3.4 %collective-permute-start.2 = (f32[384,768]{0,1:T(8,128)}, f32[384,768]{0,1:T(8,128)S(1)}, u32[]{:S(2)}, u32[]{:S(2)}) collective-permute-start(f32[384,768]{0,1:T(8,128)} %fusion.23), channel_id=1, source_target_pairs={{2,0},{4,2},{6,4},{8,6},{10,8},{12,10},{14,12},{16,14},{18,16},{20... | collective-permute-start | bytes 3538952 | tf_op jit(solution)/shard_map/ppermute | solution.py:143
  187.4 0.5 slice.122
  189.2 0.9 collective-permute-start.4
  190.1 6.3 %fusion.6 = f32[1,768,768]{2,1,0:T(8,128)} fusion(f32[16,16,768]{2,1,0:T(8,128)} %all-to-all-done, f32[]{:T(128)} %bitcast, f32[768,1536]{1,0:T(8,128)} %param.7, pred[]{:T(512)S(6)} %eq.9), kind=kOutput, calls=%fused_computation.14 | convolution fusion | flops 907739136 | bytes 8651265 | tf_op jit(solution)/shard_map/dot_general | solution.py:130
  197.0 0.5 slice.121
  198.9 1.7 fusion.41
  200.6 37.2 %collective-permute-done.2 = f32[384,768]{0,1:T(8,128)S(1)} collective-permute-done((f32[384,768]{0,1:T(8,128)}, f32[384,768]{0,1:T(8,128)S(1)}, u32[]{:S(2)}, u32[]{:S(2)}) %collective-permute-start.2) | collective-permute-done | bytes 1179680 | tf_op jit(solution)/shard_map/ppermute | solution.py:143
  237.8 0.8 slice.131
  238.7 0.9 slice.132
  239.6 0.9 slice.133
  240.5 1.0 slice.134
  241.5 1.0 slice.135
  242.6 1.0 slice_dynamic-update-slice_fusion
  243.7 2.0 copy.27
  245.7 3.4 %fusion.5 = f32[1,768,768]{2,1,0:T(8,128)} fusion(f32[768,768]{1,0:T(8,128)S(1)} %slice_dynamic-update-slice_fusion, f32[768,768]{0,1:T(8,128)} %copy.27, s32[768]{0:T(1024)S(1)} %add_select_fusion), kind=kLoop, calls=%fused_computation.11 | loop fusion | flops 1179648 | bytes 7080960 | tf_op jit(solution)/shard_map/concatenate | solution.py:214
  249.1 0.0 collective-permute-done.3
  249.1 2.9 %pad_maximum_fusion = f32[768,768]{0,1:T(8,128)} fusion(f32[384,768]{0,1:T(8,128)} %collective-permute-done.3, f32[384,768]{0,1:T(8,128)S(1)} %collective-permute-done.2), kind=kLoop, calls=%fused_computation.6 | loop fusion | flops 589824 | bytes 4718592 | tf_op jit(solution)/shard_map/concatenate | solution.py:208
  252.0 2.0 copy.29
  254.1 0.0 copy-start.5
  254.1 0.0 copy-start.6
  254.1 1.7 fusion.4
  255.8 0.3 copy-done.4
  256.1 0.7 copy-done.5
  256.8 0.7 copy-done.6
  257.5 9.9 %fusion.2 = (f32[1,768,1536]{2,1,0:T(8,128)}, f32[1,768,1536]{2,1,0:T(8,128)}) fusion(f32[1,768,768]{2,1,0:T(8,128)S(1)} %copy-done.6, f32[1,768,768]{2,1,0:T(8,128)S(1)} %bitcast.64, f32[]{:T(128)} %bitcast.21, pred[]{:T(512)S(6)} %eq.9, f32[1,768,768]{2,1,0:T(8,128)} %fusion.5, f32[1,768,768]{2,1,0:T(8,128)S(1)} %fusion.4, f32[]{:T(128)} %bitcast.9, ...), kind=kLoop, calls=%fused_computation.5 | loop fusion | flops 15335424 | bytes 23592968 | tf_op jit(solution)/shard_map/mul | solution.py:221
  (24 shorter events, 0.2 us)
Async XLA Ops:
  1.5 1.4 copy-start
  2.9 0.7 copy-start.1
  4.3 8.6 %copy-start.10 = (f32[2]{0:T(128)S(1)}, f32[2]{0:T(128)}, u32[]{:S(2)}) copy-start(f32[2]{0:T(128)} %param.9) | copy-start | bytes 28
  5.6 25.7 %all-to-all-start.1 = ((f32[16,16,768]{2,1,0:T(8,128)}), f32[16,16,768]{2,1,0:T(8,128)S(1)}, u32[]{:S(2)}, u32[]{:S(2)}) async-start(f32[16,16,768]{2,1,0:T(8,128)} %get-tuple-element.17), calls=%async_computation.1 | async-start | bytes 1572864 | tf_op jit(solution)/shard_map/all_to_all | solution.py:179
  36.0 1.4 copy-start.7
  89.7 11.5 %copy-start.11 = (f32[2]{0:T(128)S(1)}, f32[2]{0:T(128)}, u32[]{:S(2)}) copy-start(f32[2]{0:T(128)} %param.10) | copy-start | bytes 28
  95.1 7.9 %collective-permute-start = (f32[768,768]{1,0:T(8,128)}, f32[768,768]{1,0:T(8,128)}, u32[]{:S(2)}, u32[]{:S(2)}) collective-permute-start(f32[768,768]{1,0:T(8,128)} %fusion.14), channel_id=1, source_target_pairs={{0,1},{1,0},{2,3},{3,2},{4,5},{5,4},{6,7},{7,6},{8,9},{9,8},{10,11... | collective-permute-start | bytes 7077896 | tf_op jit(solution)/shard_map/ppermute | solution.py:191
  95.1 95.1 %all-to-all-start = ((f32[16,16,768]{2,1,0:T(8,128)}), f32[16,16,768]{2,1,0:T(8,128)}, u32[]{:S(2)}, u32[]{:S(2)}) async-start(f32[16,16,768]{2,1,0:T(8,128)} %get-tuple-element.18), calls=%async_computation | async-start | bytes 1572864 | tf_op jit(solution)/shard_map/all_to_all | solution.py:179
  103.0 6.3 %copy-start.9 = (f32[1536]{0:T(1024)S(1)}, f32[1536]{0:T(1024)}, u32[]{:S(2)}) copy-start(f32[1536]{0:T(1024)} %param.8) | copy-start | bytes 18436
  162.7 1.5 copy-start.8
  169.0 1.4 copy-start.2
  170.4 3.9 %slice-start = ((f32[768,768]{1,0:T(8,128)}), f32[128,768]{1,0:T(8,128)S(1)}, s32[]{:S(2)}) async-start(f32[768,768]{1,0:T(8,128)} %copy-done.8), calls=%async_computation.2 | async-start | bytes 786432 | tf_op jit(solution)/shard_map/slice | solution.py:152
  174.3 4.7 %copy-start.3 = (f32[768,768]{1,0:T(8,128)S(1)}, f32[768,768]{1,0:T(8,128)}, u32[]{:S(2)}) copy-start(f32[768,768]{1,0:T(8,128)} %copy-done.2) | copy-start | bytes 7077892
  176.6 61.2 %collective-permute-start.1 = (f32[384,896]{1,0:T(8,128)}, f32[384,896]{1,0:T(8,128)}, u32[]{:S(2)}, u32[]{:S(2)}) collective-permute-start(f32[384,896]{1,0:T(8,128)} %maximum_multiply_fusion), channel_id=1, source_target_pairs={{2,0},{4,2},{6,4},{8,6},{10,8},{12,10},{14,12},{16,14},{18,16},{20... | collective-permute-start | bytes 4128776 | tf_op jit(solution)/shard_map/ppermute | solution.py:143
  181.6 56.2 %collective-permute-start.2 = (f32[384,768]{0,1:T(8,128)}, f32[384,768]{0,1:T(8,128)S(1)}, u32[]{:S(2)}, u32[]{:S(2)}) collective-permute-start(f32[384,768]{0,1:T(8,128)} %fusion.23), channel_id=1, source_target_pairs={{2,0},{4,2},{6,4},{8,6},{10,8},{12,10},{14,12},{16,14},{18,16},{20... | collective-permute-start | bytes 3538952 | tf_op jit(solution)/shard_map/ppermute | solution.py:143
  189.2 9.0 %collective-permute-start.4 = (f32[1]{0:T(128)}, f32[1]{0:T(128)}, u32[]{:S(2)}, u32[]{:S(2)}) collective-permute-start(f32[1]{0:T(128)} %bitcast.25), channel_id=1, source_target_pairs={{0,1},{1,0},{2,3},{3,2},{4,5},{5,4},{6,7},{7,6},{8,9},{9,8},{10,11... | collective-permute-start | bytes 20 | tf_op jit(solution)/shard_map/ppermute | solution.py:195
  237.8 11.3 %collective-permute-start.3 = (f32[384,768]{0,1:T(8,128)S(1)}, f32[384,768]{0,1:T(8,128)}, u32[]{:S(2)}, u32[]{:S(2)}) collective-permute-start(f32[384,768]{0,1:T(8,128)S(1)} %collective-permute-done.2), channel_id=1, source_target_pairs={{0,1},{1,0},{2,3},{3,2},{4,5},{5,4},{6,7},{7,6},{8,9},{9,8},{10,11... | collective-permute-start | bytes 3538952 | tf_op jit(solution)/shard_map/ppermute | solution.py:205
  254.0 2.0 copy-start.4
  254.1 2.7 %copy-start.5 = (f32[1,768,768]{2,1,0:T(8,128)S(1)}, f32[1,768,768]{2,1,0:T(8,128)}, u32[]{:S(2)}) copy-start(f32[1,768,768]{2,1,0:T(8,128)} %get-tuple-element.13) | copy-start | bytes 7077892
  254.1 3.4 %copy-start.6 = (f32[1,768,768]{2,1,0:T(8,128)S(1)}, f32[1,768,768]{2,1,0:T(8,128)}, u32[]{:S(2)}) copy-start(f32[1,768,768]{2,1,0:T(8,128)} %fusion.41) | copy-start | bytes 7077892
